TPU v7x, 32 devices: a whole 2x2x4 slice. The times are simulated.
32 devices in a mesh: row: 8 (over y, x, core), col: 4 (over z).
Axes of the slice: x: 2, y: 2, z: 4, core: 2. Of those that a mesh axis runs over, the one named last changes fastest.
Arguments:
- density: bfloat16 [4096, 4096], P('row', 'col'), as said below
- pattern: int32 [64, 64], P('row', 'col'), may hold values from 0 to 1, as said below
Outputs:
- updated: bfloat16 [4096, 4096], P('row', 'col')
- occupations: float32 [2], replicated
Inputs may be any that keep to these rules, and one draw needn't show every extreme that they name: pattern is symmetric, every diagonal block is 1. density is exactly symmetric and zero wherever pattern is 0.
All inputs are finite; a program needn't handle non-finite values.
Results may differ from a plain program's by a relative error of at most 0.0015.
Values may be sent and summed in bfloat16 or wider, within the bound.
A program may use at most 64 MiB of HBM per device.

v0:
```python
import jax
import jax.numpy as jnp
from jax import lax
from jax.sharding import PartitionSpec as P

BLK = 64


def expand_blocks(block_mask, width):
    block_rows, block_cols = block_mask.shape
    grid = jnp.broadcast_to(
        block_mask.astype(jnp.float32)[:, None, :, None], (block_rows, width, block_cols, width)
    )
    return grid.reshape(block_rows * width, block_cols * width)


def body(density, pattern):
    slab_rows, slab_cols = density.shape
    cell_mask = expand_blocks(pattern, BLK)
    column_panel = lax.all_gather(density, "row", axis=0, tiled=True)
    row_offset = lax.axis_index("row") * slab_rows
    col_offset = lax.axis_index("col") * slab_cols
    global_rows = row_offset + lax.iota(jnp.int32, slab_rows)
    global_cols = col_offset + lax.iota(jnp.int32, slab_cols)
    on_diagonal = global_rows[:, None] == global_cols[None, :]
    density_wide = density.astype(jnp.float32)
    trace_p_part = jnp.sum(jnp.where(on_diagonal, density_wide, 0.0))
    square = jnp.dot(
        lax.all_gather(density, "col", axis=1, tiled=True),
        column_panel,
        preferred_element_type=jnp.float32,
    )
    square = square * cell_mask
    trace_c_part = jnp.sum(jnp.where(on_diagonal, square, 0.0))
    trace_p, trace_c = lax.psum((trace_p_part, trace_c_part), ("row", "col"))
    order_total = slab_rows * lax.axis_size("row")
    take_square = trace_p > 1.0 * order_total
    updated = jnp.where(take_square, square, cell_mask * (2.0 * density_wide - square))
    trace_new = jnp.where(take_square, trace_c, 2.0 * trace_p - trace_c)
    occupations = jnp.stack([trace_p, trace_new]) / order_total
    return (updated.astype(jnp.bfloat16), occupations)


def solution(mesh):
    placed = (P("row", "col"), P("row", "col"))
    return jax.shard_map(
        body, mesh=mesh, in_specs=placed, out_specs=(P("row", "col"), P()), check_vma=False
    )
```

profile of v0, /device:TPU:7, one launch (start us, length us, event | category | flops | bytes accessed | tf_op | source)
XLA Modules:
  0.0 210.2 jit_solution(5599611315656936817)
XLA Ops:
  7.2 0.0 copy-start.1
  7.2 0.0 all-gather.3.cloned.1.call-start
  7.2 0.7 all-gather.3.cloned.1.call-update
  7.9 0.0 all-gather.5.cloned.1.call-start
  8.0 0.7 all-gather.5.cloned.1.call-update
  8.7 0.0 copy-done.1
  8.7 2.3 %broadcast_in_dim.14 = f32[8,64,16,64]{3,2,1,0:T(8,128)} broadcast(f32[8,16]{1,0:T(8,128)S(1)} %convert_element_type.10), dimensions={0,2} | broadcast | bytes 2097664 | tf_op jit(solution)/shard_map/broadcast_in_dim | solution.py:11
  11.0 0.0 copy-start
  11.0 3.6 %reshape.16 = f32[512,1024]{1,0:T(8,128)S(1)} reshape(f32[8,64,16,64]{3,2,1,0:T(8,128)} %broadcast_in_dim.14) | data formatting | bytes 4194304 | tf_op jit(solution)/shard_map/reshape | solution.py:14
  14.6 77.0 %all-gather.3.cloned.1.call-done = bf16[512,4096]{1,0:T(8,128)(2,1)} async-done(((bf16[512,1024]{1,0:T(8,128)(2,1)}), bf16[512,4096]{1,0:T(8,128)(2,1)}) %all-gather.3.cloned.1.call-update) | async-done | bytes 4194320 | tf_op jit(solution)/shard_map/all_gather | solution.py:29
  91.6 54.3 %all-gather.5.cloned.1.call-done = bf16[4096,1024]{1,0:T(8,128)(2,1)} async-done(((bf16[512,1024]{1,0:T(8,128)(2,1)}), bf16[4096,1024]{1,0:T(8,128)(2,1)}) %all-gather.5.cloned.1.call-update) | async-done | bytes 8388624 | tf_op jit(solution)/shard_map/all_gather | solution.py:20
  145.9 0.0 copy-done
  145.9 11.1 %fusion.5 = (f32[]{:T(128)}, f32[]{:T(128)}, f32[512,1024]{1,0:T(8,128)}) fusion(f32[512,1024]{1,0:T(8,128)S(1)} %reshape.16, s32[1024]{0:T(1024)S(1)} %iota_add_fusion, s32[512]{0:T(512)S(1)} %iota_add_fusion.1, bf16[512,1024]{1,0:T(8,128)(2,1)S(1)} %copy-done, bf16[512,4096]{1,0:T(8,128)(2,1)} %all-gather.3.cloned.1.call-done, ...), kind=kOutput, calls=%fused_computation.8 | convolution fusion | flops 4298637312 | bytes 17831944 | tf_op jit(solution)/shard_map/dot_general | solution.py:28
  157.0 39.4 %all-reduce = (f32[]{:T(128)}, f32[]{:T(128)}) all-reduce(f32[]{:T(128)} %get-tuple-element.3, f32[]{:T(128)} %get-tuple-element.2), channel_id=1, replica_groups=mesh['row'=8,'col'=4] {'row','col'}, use_global_device_ids=true, to_apply=%region_1.2 | all-reduce | flops 2 | bytes 16 | tf_op jit(solution)/shard_map/psum | solution.py:35
  198.9 3.2 %fusion.3 = bf16[512,1024]{1,0:T(8,128)(2,1)} fusion(f32[512,1024]{1,0:T(8,128)S(1)} %reshape.16, bf16[512,1024]{1,0:T(8,128)(2,1)S(1)} %copy-done, f32[512,1024]{1,0:T(8,128)} %get-tuple-element.6, pred[]{:T(512)S(6)} %gt.3), kind=kLoop, calls=%fused_computation.6 | loop fusion | flops 3670016 | bytes 6291457 | tf_op jit(solution)/shard_map/convert_element_type | solution.py:41
  202.1 1.2 maximum_multiply_fusion
  (3 shorter events, 0.0 us)
Async XLA Ops:
  7.2 1.5 copy-start.1
  7.2 84.4 %all-gather.3.cloned.1.call-start = ((), (), s32[]{:S(2)}) async-start(), calls=%async_computation | async-start | bytes 5242880 | tf_op jit(solution)/shard_map/all_gather | solution.py:29
  7.9 138.0 %all-gather.5.cloned.1.call-start = ((), (), s32[]{:S(2)}) async-start(), calls=%async_computation.1 | async-start | bytes 9437184 | tf_op jit(solution)/shard_map/all_gather | solution.py:20
  11.0 134.9 %copy-start = (bf16[512,1024]{1,0:T(8,128)(2,1)S(1)}, bf16[512,1024]{1,0:T(8,128)(2,1)}, u32[]{:S(2)}) copy-start(bf16[512,1024]{1,0:T(8,128)(2,1)} %param.2) | copy-start | bytes 3145732
Sparse Core Ops, SparseCore 0:
  9.6 81.9 all-gather.2
  93.5 52.3 all-gather.4
where the time goes:
time: 213 us; the launch traced here: 210 us
  waiting for transfers between devices  133 us (62%)
  blocking collectives  39.4 us (18%)
  between operations  16.7 us (8%)
  matrix products  11.1 us (5%)
  local copies, waits for them, and re-layouts  5.88 us (3%)
  other arithmetic  4.4 us (2%)
    all_gather x1, waiting for transfers between devices, body(): lax.all_gather(density, 'col', axis=1, tiled=True)  77 us
    all_gather x1, waiting for transfers between devices, body(): column_panel = lax.all_gather(density, 'row', axis=0, tiled=True)  54.3 us
    psum x1, blocking collectives, body(): trace_p, trace_c = lax.psum((trace_p_part, trace_c_part), ('row', 'col'))  39.4 us
    dot_general x1, matrix products, body(): jnp.dot(lax.all_gather(density, 'col', axis=1, tiled=True), column_panel,...  11.1 us
  transfers between devices with their start and end apart: 2, of which 2 were waited for; matrix products, arithmetic and copies ran while one was open for 3% of the time, Pallas kernels for 0%

commit v1 on v0

--- a/solution.py
+++ b/solution.py
@@ -1,9 +1,15 @@
+import functools
+
 import jax
 import jax.numpy as jnp
 from jax import lax
+from jax.experimental import pallas as pl
+from jax.experimental.pallas import tpu as pltpu
 from jax.sharding import PartitionSpec as P
 
 BLK = 64
+MESH = pl.DeviceIdType.MESH
+NCH = 4
 
 
 def expand_blocks(block_mask, width):
@@ -14,7 +20,7 @@
     return grid.reshape(block_rows * width, block_cols * width)
 
 
-def body(density, pattern):
+def plain_body(density, pattern):
     slab_rows, slab_cols = density.shape
     cell_mask = expand_blocks(pattern, BLK)
     column_panel = lax.all_gather(density, "row", axis=0, tiled=True)
@@ -41,8 +47,268 @@
     return (updated.astype(jnp.bfloat16), occupations)
 
 
+def kernel(order_total, p_ref, pat_ref, out_ref, occ_ref, arow, bcol, acc, tz, tp, tsum,
+           up_s, up_r, dn_s, dn_r, x_s, x_r, y_s, y_r, s_s, s_r, tz_s, tz_r, tp_s, tp_r):
+    rows, cols = p_ref.shape
+    ch = rows // NCH
+    r = lax.axis_index("row")
+    c = lax.axis_index("col")
+    core = r % 2
+    x = (r // 2) % 2
+    y = r // 4
+    sib = r + 1 - 2 * core
+    xn = r + 2 - 4 * x
+    yn = r + 4 - 8 * y
+    dg = xn + 4 - 8 * y
+
+    barrier = pltpu.get_barrier_semaphore()
+    for d in range(1, 8):
+        pl.semaphore_signal(barrier, inc=1, device_id=((r + d) % 8, c), device_id_type=MESH)
+    for d in range(1, 4):
+        pl.semaphore_signal(barrier, inc=1, device_id=(r, (c + d) % 4), device_id_type=MESH)
+    pl.semaphore_wait(barrier, 10)
+
+    def send(src, dst, ss, rs, dev):
+        return pltpu.make_async_remote_copy(
+            src_ref=src, dst_ref=dst, send_sem=ss, recv_sem=rs, device_id=dev, device_id_type=MESH
+        )
+
+    def piece(k):
+        return pl.ds(k * ch, ch) if isinstance(k, int) else pl.ds(pl.multiple_of(k * ch, ch), ch)
+
+    def z_up(slot, own, k):
+        src = p_ref if own else arow.at[slot]
+        pos = k
+        return send(src.at[piece(k % NCH)], arow.at[slot, piece(k % NCH)],
+                    up_s.at[pos], up_r.at[pos], (r, (c + 1) % 4))
+
+    def z_dn(slot, own, k):
+        src = p_ref if own else arow.at[slot]
+        return send(src.at[piece(k % NCH)], arow.at[slot, piece(k % NCH)],
+                    dn_s.at[k], dn_r.at[k], (r, (c + 3) % 4))
+
+    def x_own(k):
+        return send(p_ref.at[piece(k)], bcol.at[r, piece(k)], x_s.at[k], x_r.at[k], (xn, c))
+
+    def y_own(k):
+        return send(p_ref.at[piece(k)], bcol.at[r, piece(k)], y_s.at[k], y_r.at[k], (yn, c))
+
+    def y_fwd(k):
+        return send(bcol.at[xn, piece(k)], bcol.at[xn, piece(k)], y_s.at[4 + k], y_r.at[4 + k], (yn, c))
+
+    def x_fwd(k):
+        return send(bcol.at[yn, piece(k)], bcol.at[yn, piece(k)], x_s.at[2 + k], x_r.at[2 + k], (xn, c))
+
+    def sib_fwd(slot, k, pos, own=False):
+        src = p_ref if own else bcol.at[slot]
+        return send(src.at[piece(k)], bcol.at[slot, piece(k)], s_s.at[pos], s_r.at[pos], (sib, c))
+
+    def got(ref, sem):
+        send(ref, ref, sem, sem, (sib, c)).wait_recv()
+
+    for k in range(NCH):
+        @pl.when(c < 3)
+        def _(k=k):
+            z_up(c, True, k).start()
+
+        @pl.when(c > 0)
+        def _(k=k):
+            z_dn(c, True, k).start()
+
+        x_own(k).start()
+        y_own((k + 2) % NCH).start()
+    for k in range(NCH):
+        sib_fwd(r, k, k, True).start()
+
+    def part(i, carry):
+        tpp, tcc = carry
+        start = pl.multiple_of(i * 64, 64)
+        v = p_ref[pl.ds(start, 64), :]
+        arow[c, pl.ds(start, 64), :] = v
+        bcol[r, pl.ds(start, 64), :] = v
+        w = v.astype(jnp.float32)
+        gr = lax.broadcasted_iota(jnp.int32, w.shape, 0) + (r * rows + start)
+        gc = lax.broadcasted_iota(jnp.int32, w.shape, 1) + c * cols
+        dpart = jnp.where(gr == gc, w, 0.0)
+        return tpp + jnp.sum(dpart, axis=0, keepdims=True), tcc + jnp.sum(w * w, axis=0, keepdims=True)
+
+    zero = jnp.zeros((1, cols), jnp.float32)
+    tpp, tcc = lax.fori_loop(0, rows // 64, part, (zero, zero))
+    which = lax.broadcasted_iota(jnp.int32, (8, 128), 0)
+    tz[c] = jnp.where(which == 0, jnp.sum(tpp), jnp.sum(tcc))
+    tz_out = [send(tz.at[c], tz.at[c], tz_s.at[d], tz_r.at[d], (r, (c + d) % 4)) for d in range(1, 4)]
+    for t in tz_out:
+        t.start()
+
+    def z_step(i):
+        @pl.when(i < NCH * c)
+        def _():
+            slot = c - 1 - i // NCH
+            got(arow.at[slot, piece(i % NCH)], up_r.at[i])
+
+            @pl.when(c < 3)
+            def _():
+                k = i + NCH
+                send(arow.at[slot, piece(i % NCH)], arow.at[slot, piece(i % NCH)],
+                     up_s.at[k], up_r.at[k], (r, (c + 1) % 4)).start()
+
+        @pl.when(i < NCH * (3 - c))
+        def _():
+            slot = c + 1 + i // NCH
+            got(arow.at[slot, piece(i % NCH)], dn_r.at[i])
+
+            @pl.when(c > 0)
+            def _():
+                k = i + NCH
+                send(arow.at[slot, piece(i % NCH)], arow.at[slot, piece(i % NCH)],
+                     dn_s.at[k], dn_r.at[k], (r, (c + 3) % 4)).start()
+
+    for i in range(6):
+        if i < 4:
+            kx, ky = i, (i + 2) % NCH
+            got(bcol.at[xn, piece(kx)], x_r.at[kx])
+            if kx < 2:
+                y_fwd(kx).start()
+            sib_fwd(xn, kx, 4 + kx).start()
+            got(bcol.at[yn, piece(ky)], y_r.at[ky])
+            if ky >= 2:
+                x_fwd(ky).start()
+            sib_fwd(yn, ky, 8 + ky).start()
+        else:
+            k = i - 4
+            got(bcol.at[dg, piece(2 + k)], x_r.at[4 + k])
+            sib_fwd(dg, 2 + k, 14 + k).start()
+            got(bcol.at[dg, piece(k)], y_r.at[4 + k])
+            sib_fwd(dg, k, 12 + k).start()
+        z_step(i)
+        if i == 1:
+            for t in tz_out:
+                t.wait_send()
+            for d in range(1, 4):
+                got(tz.at[(c + 4 - d) % 4], tz_r.at[d])
+            tp[r] = ((tz[0] + tz[1]) + tz[2]) + tz[3]
+            tp_out = [send(tp.at[r], tp.at[r], tp_s.at[d], tp_r.at[d], ((r + d) % 8, c)) for d in range(1, 8)]
+            for t in tp_out:
+                t.start()
+
+    sr = sib
+    sx, sy, sd = xn + 1 - 2 * core, yn + 1 - 2 * core, dg + 1 - 2 * core
+    for slot, base in ((sr, 0), (sx, 4), (sy, 8), (sd, 12)):
+        for k in range(NCH):
+            got(bcol.at[slot, piece(k)], s_r.at[base + k])
+    z_step(6)
+
+    def mm(slot, k, first=False):
+        rr = piece(k)
+        a = arow[slot, rr, :]
+        half = cols // 2
+        v = jnp.dot(a[:, :half], bcol[2 * slot], preferred_element_type=jnp.float32)
+        v += jnp.dot(a[:, half:], bcol[2 * slot + 1], preferred_element_type=jnp.float32)
+        acc[rr, :] = v if first else acc[rr, :] + v
+
+    def own_mm(k, _):
+        mm(c, k, True)
+        return 0
+
+    lax.fori_loop(0, NCH, own_mm, 0)
+    z_step(7)
+
+    def near(i, _):
+        @pl.when(i < NCH * c)
+        def _():
+            mm(c - 1 - i // NCH, i % NCH)
+
+        @pl.when(i < NCH * (3 - c))
+        def _():
+            mm(c + 1 + i // NCH, i % NCH)
+        return 0
+
+    def tail(i, _):
+        z_step(i)
+        near(i - NCH, 0)
+        return 0
+
+    lax.fori_loop(0, NCH, near, 0)
+    lax.fori_loop(2 * NCH, 3 * NCH, tail, 0)
+    lax.fori_loop(2 * NCH, 3 * NCH, near, 0)
+
+    for t in tp_out:
+        t.wait_send()
+    for d in range(1, 8):
+        got(tp.at[(r + 8 - d) % 8], tp_r.at[d])
+    tot = tp[0]
+    for d in range(1, 8):
+        tot = tot + tp[d]
+    tsum[...] = tot
+    sel = lax.broadcasted_iota(jnp.int32, (8, 128), 1) == 0
+    trace_p = jnp.sum(jnp.where(sel & (which == 0), tot, 0.0))
+    trace_c = jnp.sum(jnp.where(sel & (which == 1), tot, 0.0))
+    take = trace_p > 1.0 * order_total
+    occ_ref[0] = trace_p / order_total
+    occ_ref[1] = jnp.where(take, trace_c, 2.0 * trace_p - trace_c) / order_total
+    takev = tsum[0:1, 0:1] > 1.0 * order_total
+
+    nbr, nbc = pat_ref.shape
+    spread = (lax.broadcasted_iota(jnp.int32, (nbc, cols), 1) // BLK
+              == lax.broadcasted_iota(jnp.int32, (nbc, cols), 0)).astype(jnp.float32)
+    mask = jnp.dot(pat_ref[...].astype(jnp.float32), spread, preferred_element_type=jnp.float32)
+    for b in range(nbr):
+        rr = pl.ds(b * BLK, BLK)
+        m = mask[b:b + 1, :]
+        sq = acc[rr, :] * m
+        alt = m * (2.0 * p_ref[rr, :].astype(jnp.float32) - sq)
+        out_ref[rr, :] = jnp.where(takev, sq, alt).astype(jnp.bfloat16)
+
+    for k in range(NCH):
+        x_own(k).wait_send()
+        y_own(k).wait_send()
+    for k in range(2):
+        y_fwd(k).wait_send()
+        x_fwd(2 + k).wait_send()
+    for pos in range(16):
+        sib_fwd(r, 0, pos, True).wait_send()
+    for i in range(4 * NCH - 4):
+        @pl.when((c < 3) & (i < NCH * (c + 1)))
+        def _(i=i):
+            z_up(c, True, i).wait_send()
+
+        @pl.when((c > 0) & (i < NCH * (4 - c)))
+        def _(i=i):
+            z_dn(c, True, i).wait_send()
+
+
+def body(density, pattern):
+    rows, cols = density.shape
+    order_total = rows * lax.axis_size("row")
+    dma = pltpu.SemaphoreType.DMA
+    return pl.pallas_call(
+        functools.partial(kernel, order_total),
+        out_shape=(jax.ShapeDtypeStruct((rows, cols), jnp.bfloat16),
+                   jax.ShapeDtypeStruct((2,), jnp.float32)),
+        in_specs=[pl.BlockSpec(memory_space=pltpu.VMEM)] * 2,
+        out_specs=(pl.BlockSpec(memory_space=pltpu.VMEM), pl.BlockSpec(memory_space=pltpu.SMEM)),
+        scratch_shapes=[
+            pltpu.VMEM((4, rows, cols), jnp.bfloat16),
+            pltpu.VMEM((8, rows, cols), jnp.bfloat16),
+            pltpu.VMEM((rows, cols), jnp.float32),
+            pltpu.VMEM((4, 8, 128), jnp.float32),
+            pltpu.VMEM((8, 8, 128), jnp.float32),
+            pltpu.VMEM((8, 128), jnp.float32),
+            dma((12,)), dma((12,)), dma((12,)), dma((12,)),
+            dma((6,)), dma((6,)), dma((6,)), dma((6,)),
+            dma((16,)), dma((16,)),
+            dma((4,)), dma((4,)), dma((8,)), dma((8,)),
+        ],
+        compiler_params=pltpu.CompilerParams(
+            collective_id=0, has_side_effects=True, vmem_limit_bytes=40 * 2**20
+        ),
+    )(density, pattern)
+
+
 def solution(mesh):
     placed = (P("row", "col"), P("row", "col"))
+    fits = mesh.shape["row"] == 8 and mesh.shape["col"] == 4
     return jax.shard_map(
-        body, mesh=mesh, in_specs=placed, out_specs=(P("row", "col"), P()), check_vma=False
+        body if fits else plain_body, mesh=mesh, in_specs=placed,
+        out_specs=(P("row", "col"), P()), check_vma=False
     )

time: 213 us -> 83.3 us (0.39)
  the two profiles are of different devices: /device:TPU:7 before, /device:TPU:0 now
where the time goes in v1:
time: 83.3 us; the launch traced here: 83.1 us
  Pallas kernels  79.1 us (95%)
  local copies, waits for them, and re-layouts  3.39 us (4%)
    pallas_call x1, Pallas kernels, body(): pl.pallas_call(functools.partial(kernel, order_total), out_shape=(jax.Sha...  79.1 us
    unnamed x6, local copies, waits for them, and re-layouts  3.39 us

profile of v1, /device:TPU:0, one launch (start us, length us, event | category | flops | bytes accessed | tf_op | source)
XLA Modules:
  0.0 83.1 jit_solution(17573484426862875115)
XLA Ops:
  0.6 0.0 copy-start
  0.6 1.2 %copy-done = bf16[512,1024]{1,0:T(8,128)(2,1)S(1)} copy-done((bf16[512,1024]{1,0:T(8,128)(2,1)S(1)}, bf16[512,1024]{1,0:T(8,128)(2,1)}, u32[]{:S(2)}) %copy-start) | copy-done | bytes 1048600
  1.9 0.0 copy-start.1
  1.9 0.7 copy-done.1
  2.5 79.1 %shard_map.41 = (bf16[512,1024]{1,0:T(8,128)(2,1)S(1)}, f32[2]{0:T(128)S(1)}) custom-call(bf16[512,1024]{1,0:T(8,128)(2,1)S(1)} %copy-done, s32[8,16]{1,0:T(8,128)S(1)} %copy-done.1), custom_call_target="tpu_custom_call" | custom-call | tf_op jit(solution)/shard_map/pallas_call | solution.py:284
  81.6 1.0 %copy.6 = bf16[512,1024]{1,0:T(8,128)(2,1)} copy(bf16[512,1024]{1,0:T(8,128)(2,1)S(1)} %get-tuple-element.4) | data formatting | bytes 2097152
  82.6 0.5 copy.7
Async XLA Ops:
  0.6 1.2 %copy-start = (bf16[512,1024]{1,0:T(8,128)(2,1)S(1)}, bf16[512,1024]{1,0:T(8,128)(2,1)}, u32[]{:S(2)}) copy-start(bf16[512,1024]{1,0:T(8,128)(2,1)} %p_ref.1) | copy-start | bytes 3145732
  1.9 0.7 copy-start.1

commit v2 on v1

--- a/solution.py
+++ b/solution.py
@@ -47,10 +47,12 @@
     return (updated.astype(jnp.bfloat16), occupations)
 
 
-def kernel(order_total, p_ref, pat_ref, out_ref, occ_ref, arow, bcol, acc, tz, tp, tsum,
-           up_s, up_r, dn_s, dn_r, x_s, x_r, y_s, y_r, s_s, s_r, tz_s, tz_r, tp_s, tp_r):
+def kernel(order_total, p_ref, pat_ref, out_ref, occ_ref, arow, bcol, acc, xa, xb, tz, tp, tsum,
+           mid_s, mid_r, inn_s, inn_r, edge_s, edge_r, dia_s, xa_r, xb_r, fa_s, fb_s,
+           x_s, x_r, y_s, y_r, s_s, s_r, tz_s, tz_r, tp_s, tp_r):
     rows, cols = p_ref.shape
     ch = rows // NCH
+    half = cols // 2
     r = lax.axis_index("row")
     c = lax.axis_index("col")
     core = r % 2
@@ -60,6 +62,17 @@
     xn = r + 2 - 4 * x
     yn = r + 4 - 8 * y
     dg = xn + 4 - 8 * y
+    flip = c // 2
+    chip = r // 2
+    role = chip + flip * (3 - 2 * chip)
+    is_mid = (c == 1) | (c == 2)
+    is_end = (c == 0) | (c == 3)
+    inward = (c + 1 - 2 * flip) % 4
+    outward = (c + 3 + 2 * flip) % 4
+    zhalf = jnp.where(role == 3, core, 1 - core)
+
+    def blk(b):
+        return b + flip * (3 - 2 * b)
 
     barrier = pltpu.get_barrier_semaphore()
     for d in range(1, 8):
@@ -73,19 +86,86 @@
             src_ref=src, dst_ref=dst, send_sem=ss, recv_sem=rs, device_id=dev, device_id_type=MESH
         )
 
+    def got(ref, sem):
+        send(ref, ref, sem, sem, (sib, c)).wait_recv()
+
+    def start(t):
+        t.start()
+
+    def drain(t):
+        t.wait_send()
+
     def piece(k):
         return pl.ds(k * ch, ch) if isinstance(k, int) else pl.ds(pl.multiple_of(k * ch, ch), ch)
 
-    def z_up(slot, own, k):
-        src = p_ref if own else arow.at[slot]
-        pos = k
-        return send(src.at[piece(k % NCH)], arow.at[slot, piece(k % NCH)],
-                    up_s.at[pos], up_r.at[pos], (r, (c + 1) % 4))
-
-    def z_dn(slot, own, k):
-        src = p_ref if own else arow.at[slot]
-        return send(src.at[piece(k % NCH)], arow.at[slot, piece(k % NCH)],
-                    dn_s.at[k], dn_r.at[k], (r, (c + 3) % 4))
+    def lane(h):
+        return pl.ds(pl.multiple_of(h * half, half), half)
+
+    def inn(k):
+        return send(p_ref.at[piece(k)], arow.at[c, piece(k)], inn_s.at[k], inn_r.at[k], (r, inward))
+
+    def mid(pos):
+        src = p_ref if pos < NCH else arow.at[blk(0)]
+        slot = blk(1) if pos < NCH else blk(0)
+        k = pos % NCH
+        return send(src.at[piece(k)], arow.at[slot, piece(k)], mid_s.at[pos], mid_r.at[pos], (r, inward))
+
+    def edge(d, k, act):
+        pos = (d - 1) * NCH + k
+        src = p_ref if d == 1 else arow.at[blk(d)]
+
+        @pl.when(role == d)
+        def _():
+            act(send(src.at[piece(k)], arow.at[blk(d), piece(k)],
+                     edge_s.at[pos], edge_r.at[pos], (r, outward)))
+
+        @pl.when((role != d) & (role != 0))
+        def _():
+            act(send(src.at[piece(k), lane(zhalf)], arow.at[blk(d), piece(k), lane(zhalf)],
+                     edge_s.at[pos], edge_r.at[pos], (r, outward)))
+
+    def edge_got(d, k):
+        pos = (d - 1) * NCH + k
+
+        @pl.when(role == d)
+        def _():
+            got(arow.at[blk(d), piece(k)], edge_r.at[pos])
+
+        @pl.when((role != d) & (role != 0))
+        def _():
+            got(arow.at[blk(d), piece(k), lane(zhalf)], edge_r.at[pos])
+
+        if d < 3:
+            @pl.when(role == 3)
+            def _():
+                share_far(d, k).start()
+        else:
+            @pl.when(role == 1)
+            def _():
+                share_near(1, k).start()
+
+            @pl.when(role == 2)
+            def _():
+                share_near(2, k).start()
+
+    def share_far(d, k):
+        sem = (fa_s if d == 1 else fb_s).at[k]
+        return send(arow.at[blk(d), piece(k), lane(zhalf)], xb.at[piece(k)], sem, xb_r.at[k],
+                    (yn if d == 1 else xn, c))
+
+    def share_near(me, k):
+        dst, sem = (xa, xa_r) if me == 1 else (xb, xb_r)
+        to = (yn if me == 1 else xn) + 1 - 2 * core
+        return send(arow.at[blk(3), piece(k), lane(zhalf)], dst.at[piece(k)], fa_s.at[k], sem.at[k], (to, c))
+
+    def dia(k):
+        return send(bcol.at[yn, piece(k), lane(core)], xa.at[piece(k)], dia_s.at[k], xa_r.at[k], (r, outward))
+
+    def dia_x(k):
+        return send(xa.at[piece(k)], xa.at[piece(k)], fa_s.at[k], xa_r.at[k], (xn, c))
+
+    def dia_y(k):
+        return send(xa.at[piece(k)], xa.at[piece(k)], fb_s.at[k], xa_r.at[k], (yn, c))
 
     def x_own(k):
         return send(p_ref.at[piece(k)], bcol.at[r, piece(k)], x_s.at[k], x_r.at[k], (xn, c))
@@ -103,17 +183,15 @@
         src = p_ref if own else bcol.at[slot]
         return send(src.at[piece(k)], bcol.at[slot, piece(k)], s_s.at[pos], s_r.at[pos], (sib, c))
 
-    def got(ref, sem):
-        send(ref, ref, sem, sem, (sib, c)).wait_recv()
-
     for k in range(NCH):
-        @pl.when(c < 3)
+        @pl.when(is_end)
         def _(k=k):
-            z_up(c, True, k).start()
-
-        @pl.when(c > 0)
+            inn(k).start()
+
+        @pl.when(is_mid)
         def _(k=k):
-            z_dn(c, True, k).start()
+            mid(k).start()
+            edge(1, k, start)
 
         x_own(k).start()
         y_own((k + 2) % NCH).start()
@@ -122,12 +200,12 @@
 
     def part(i, carry):
         tpp, tcc = carry
-        start = pl.multiple_of(i * 64, 64)
-        v = p_ref[pl.ds(start, 64), :]
-        arow[c, pl.ds(start, 64), :] = v
-        bcol[r, pl.ds(start, 64), :] = v
+        at = pl.multiple_of(i * 64, 64)
+        v = p_ref[pl.ds(at, 64), :]
+        arow[c, pl.ds(at, 64), :] = v
+        bcol[r, pl.ds(at, 64), :] = v
         w = v.astype(jnp.float32)
-        gr = lax.broadcasted_iota(jnp.int32, w.shape, 0) + (r * rows + start)
+        gr = lax.broadcasted_iota(jnp.int32, w.shape, 0) + (r * rows + at)
         gc = lax.broadcasted_iota(jnp.int32, w.shape, 1) + c * cols
         dpart = jnp.where(gr == gc, w, 0.0)
         return tpp + jnp.sum(dpart, axis=0, keepdims=True), tcc + jnp.sum(w * w, axis=0, keepdims=True)
@@ -139,29 +217,15 @@
     tz_out = [send(tz.at[c], tz.at[c], tz_s.at[d], tz_r.at[d], (r, (c + d) % 4)) for d in range(1, 4)]
     for t in tz_out:
         t.start()
-
-    def z_step(i):
-        @pl.when(i < NCH * c)
-        def _():
-            slot = c - 1 - i // NCH
-            got(arow.at[slot, piece(i % NCH)], up_r.at[i])
-
-            @pl.when(c < 3)
-            def _():
-                k = i + NCH
-                send(arow.at[slot, piece(i % NCH)], arow.at[slot, piece(i % NCH)],
-                     up_s.at[k], up_r.at[k], (r, (c + 1) % 4)).start()
-
-        @pl.when(i < NCH * (3 - c))
-        def _():
-            slot = c + 1 + i // NCH
-            got(arow.at[slot, piece(i % NCH)], dn_r.at[i])
-
-            @pl.when(c > 0)
-            def _():
-                k = i + NCH
-                send(arow.at[slot, piece(i % NCH)], arow.at[slot, piece(i % NCH)],
-                     dn_s.at[k], dn_r.at[k], (r, (c + 3) % 4)).start()
+    tp_out = [send(tp.at[r], tp.at[r], tp_s.at[d], tp_r.at[d], ((r + d) % 8, c)) for d in range(1, 8)]
+
+    def mid_step(i):
+        if i < NCH:
+            got(arow.at[blk(0), piece(i)], inn_r.at[i])
+            mid(NCH + i).start()
+        b = 2 + i // NCH
+        got(arow.at[blk(b), piece(i % NCH)], mid_r.at[i])
+        edge(b, i % NCH, start)
 
     for i in range(6):
         if i < 4:
@@ -174,63 +238,140 @@
             if ky >= 2:
                 x_fwd(ky).start()
             sib_fwd(yn, ky, 8 + ky).start()
+
+            @pl.when(is_mid & (role == 0))
+            def _():
+                dia(ky).start()
         else:
             k = i - 4
             got(bcol.at[dg, piece(2 + k)], x_r.at[4 + k])
             sib_fwd(dg, 2 + k, 14 + k).start()
             got(bcol.at[dg, piece(k)], y_r.at[4 + k])
             sib_fwd(dg, k, 12 + k).start()
-        z_step(i)
+
+        @pl.when(is_mid)
+        def _():
+            mid_step(i)
+
+        @pl.when(is_end)
+        def _():
+            edge_got(1 + i // NCH, i % NCH)
+
+        if i >= 1 and i < 5:
+            kd = (i + 1) % NCH
+
+            @pl.when(is_end & (role == 0))
+            def _():
+                got(xa.at[piece(kd)], xa_r.at[kd])
+                dia_x(kd).start()
+                dia_y(kd).start()
         if i == 1:
             for t in tz_out:
                 t.wait_send()
             for d in range(1, 4):
                 got(tz.at[(c + 4 - d) % 4], tz_r.at[d])
             tp[r] = ((tz[0] + tz[1]) + tz[2]) + tz[3]
-            tp_out = [send(tp.at[r], tp.at[r], tp_s.at[d], tp_r.at[d], ((r + d) % 8, c)) for d in range(1, 8)]
             for t in tp_out:
                 t.start()
 
-    sr = sib
     sx, sy, sd = xn + 1 - 2 * core, yn + 1 - 2 * core, dg + 1 - 2 * core
-    for slot, base in ((sr, 0), (sx, 4), (sy, 8), (sd, 12)):
+    for slot, base in ((sib, 0), (sx, 4), (sy, 8), (sd, 12)):
         for k in range(NCH):
             got(bcol.at[slot, piece(k)], s_r.at[base + k])
-    z_step(6)
-
-    def mm(slot, k, first=False):
-        rr = piece(k)
-        a = arow[slot, rr, :]
-        half = cols // 2
-        v = jnp.dot(a[:, :half], bcol[2 * slot], preferred_element_type=jnp.float32)
-        v += jnp.dot(a[:, half:], bcol[2 * slot + 1], preferred_element_type=jnp.float32)
-        acc[rr, :] = v if first else acc[rr, :] + v
-
-    def own_mm(k, _):
-        mm(c, k, True)
-        return 0
-
-    lax.fori_loop(0, NCH, own_mm, 0)
-    z_step(7)
-
-    def near(i, _):
-        @pl.when(i < NCH * c)
-        def _():
-            mm(c - 1 - i // NCH, i % NCH)
-
-        @pl.when(i < NCH * (3 - c))
-        def _():
-            mm(c + 1 + i // NCH, i % NCH)
-        return 0
-
-    def tail(i, _):
-        z_step(i)
-        near(i - NCH, 0)
-        return 0
-
-    lax.fori_loop(0, NCH, near, 0)
-    lax.fori_loop(2 * NCH, 3 * NCH, tail, 0)
-    lax.fori_loop(2 * NCH, 3 * NCH, near, 0)
+
+    def mm(b, h, first=False):
+        slot = blk(b)
+
+        def some(k, _):
+            rr = piece(k)
+            v = jnp.dot(arow[slot, rr, lane(h)], bcol[2 * slot + h], preferred_element_type=jnp.float32)
+            acc[rr, :] = v if first else acc[rr, :] + v
+            return 0
+
+        lax.fori_loop(0, NCH, some, 0)
+
+    def mm_all(b):
+        lax.fori_loop(0, 2, lambda h, _: (mm(b, h), 0)[1], 0)
+
+    def turn(src, b, h):
+        for k in range(NCH):
+            arow[blk(b), :, pl.ds(pl.multiple_of(h * half + k * ch, ch), ch)] = src(k).T
+
+    @pl.when(is_mid)
+    def _():
+        mid_step(6)
+        mm(1, 0, True)
+        mm(1, 1)
+        mid_step(7)
+        mm_all(0)
+        mm_all(2)
+        mm_all(3)
+
+    @pl.when(is_end)
+    def _():
+        edge_got(2, 2)
+        mm(0, 0, True)
+        mm(0, 1)
+        edge_got(2, 3)
+
+        @pl.when(role == 0)
+        def _():
+            def slab(t, _):
+                b, h = 1 + t // 2, t % 2
+                turn(lambda k: bcol[2 * blk(b) + h, piece(k), lane(core)], b, h)
+                mm(b, h)
+                return 0
+
+            lax.fori_loop(0, 6, slab, 0)
+
+        def all_xa():
+            for k in range(NCH):
+                got(xa.at[piece(k)], xa_r.at[k])
+
+        def all_xb():
+            for k in range(NCH):
+                got(xb.at[piece(k)], xb_r.at[k])
+
+        other = 1 - zhalf
+
+        @pl.when(role == 1)
+        def _():
+            all_xa()
+            turn(lambda k: xa[piece(k), :], 2, other)
+            all_xb()
+            turn(lambda k: xb[piece(k), :], 3, other)
+
+        @pl.when(role == 2)
+        def _():
+            all_xa()
+            arow[blk(1), :, lane(other)] = xa[...]
+            all_xb()
+            turn(lambda k: xb[piece(k), :], 3, other)
+
+        @pl.when((role == 1) | (role == 2))
+        def _():
+            mm_all(1)
+            edge_got(3, 0)
+            mm_all(2)
+            edge_got(3, 1)
+            mm(3, other)
+            edge_got(3, 2)
+            edge_got(3, 3)
+            mm(3, zhalf)
+
+        @pl.when(role == 3)
+        def _():
+            mm(1, zhalf)
+            mm(2, zhalf)
+            for k in range(NCH):
+                edge_got(3, k)
+            mm_all(3)
+            all_xa()
+            turn(lambda k: xa[piece(k), :], 1, other)
+            mm(1, other)
+            all_xb()
+            turn(lambda k: xb[piece(k), :], 2, other)
+            mm(2, other)
 
     for t in tp_out:
         t.wait_send()
@@ -267,14 +408,41 @@
         x_fwd(2 + k).wait_send()
     for pos in range(16):
         sib_fwd(r, 0, pos, True).wait_send()
-    for i in range(4 * NCH - 4):
-        @pl.when((c < 3) & (i < NCH * (c + 1)))
-        def _(i=i):
-            z_up(c, True, i).wait_send()
-
-        @pl.when((c > 0) & (i < NCH * (4 - c)))
-        def _(i=i):
-            z_dn(c, True, i).wait_send()
+
+    @pl.when(is_mid)
+    def _():
+        for pos in range(2 * NCH):
+            mid(pos).wait_send()
+        for d in range(1, 4):
+            for k in range(NCH):
+                edge(d, k, drain)
+
+        @pl.when(role == 0)
+        def _():
+            for k in range(NCH):
+                dia(k).wait_send()
+
+    @pl.when(is_end)
+    def _():
+        for k in range(NCH):
+            inn(k).wait_send()
+
+        @pl.when(role == 0)
+        def _():
+            for k in range(NCH):
+                dia_x(k).wait_send()
+                dia_y(k).wait_send()
+
+        @pl.when(role == 3)
+        def _():
+            for k in range(NCH):
+                share_far(1, k).wait_send()
+                share_far(2, k).wait_send()
+
+        @pl.when((role == 1) | (role == 2))
+        def _():
+            for k in range(NCH):
+                share_near(1, k).wait_send()
 
 
 def body(density, pattern):
@@ -291,10 +459,13 @@
             pltpu.VMEM((4, rows, cols), jnp.bfloat16),
             pltpu.VMEM((8, rows, cols), jnp.bfloat16),
             pltpu.VMEM((rows, cols), jnp.float32),
+            pltpu.VMEM((rows, cols // 2), jnp.bfloat16),
+            pltpu.VMEM((rows, cols // 2), jnp.bfloat16),
             pltpu.VMEM((4, 8, 128), jnp.float32),
             pltpu.VMEM((8, 8, 128), jnp.float32),
             pltpu.VMEM((8, 128), jnp.float32),
-            dma((12,)), dma((12,)), dma((12,)), dma((12,)),
+            dma((8,)), dma((8,)), dma((4,)), dma((4,)), dma((12,)), dma((12,)),
+            dma((4,)), dma((4,)), dma((4,)), dma((4,)), dma((4,)),
             dma((6,)), dma((6,)), dma((6,)), dma((6,)),
             dma((16,)), dma((16,)),
             dma((4,)), dma((4,)), dma((8,)), dma((8,)),

time: 83.3 us -> 75.5 us (0.906)
  the two profiles are of different devices: /device:TPU:0 before, /device:TPU:7 now
where the time goes in v2:
time: 75.5 us; the launch traced here: 75.3 us
  Pallas kernels  71.3 us (94%)
  local copies, waits for them, and re-layouts  3.39 us (4%)
    pallas_call x1, Pallas kernels, body(): pl.pallas_call(functools.partial(kernel, order_total), out_shape=(jax.Sha...  71.3 us
    unnamed x6, local copies, waits for them, and re-layouts  3.39 us

profile of v2, /device:TPU:7, one launch (start us, length us, event | category | flops | bytes accessed | tf_op | source)
XLA Modules:
  0.0 75.3 jit_solution(4488057106014877406)
XLA Ops:
  0.6 0.0 copy-start
  0.6 1.2 %copy-done = bf16[512,1024]{1,0:T(8,128)(2,1)S(1)} copy-done((bf16[512,1024]{1,0:T(8,128)(2,1)S(1)}, bf16[512,1024]{1,0:T(8,128)(2,1)}, u32[]{:S(2)}) %copy-start) | copy-done | bytes 1048600
  1.9 0.0 copy-start.1
  1.9 0.7 copy-done.1
  2.5 71.3 %shard_map.41 = (bf16[512,1024]{1,0:T(8,128)(2,1)S(1)}, f32[2]{0:T(128)S(1)}) custom-call(bf16[512,1024]{1,0:T(8,128)(2,1)S(1)} %copy-done, s32[8,16]{1,0:T(8,128)S(1)} %copy-done.1), custom_call_target="tpu_custom_call" | custom-call | tf_op jit(solution)/shard_map/pallas_call | solution.py:452
  73.8 1.0 %copy.6 = bf16[512,1024]{1,0:T(8,128)(2,1)} copy(bf16[512,1024]{1,0:T(8,128)(2,1)S(1)} %get-tuple-element.4) | data formatting | bytes 2097152
  74.8 0.5 copy.7
Async XLA Ops:
  0.6 1.2 %copy-start = (bf16[512,1024]{1,0:T(8,128)(2,1)S(1)}, bf16[512,1024]{1,0:T(8,128)(2,1)}, u32[]{:S(2)}) copy-start(bf16[512,1024]{1,0:T(8,128)(2,1)} %p_ref.1) | copy-start | bytes 3145732
  1.9 0.7 copy-start.1

commit v3 on v2

--- a/solution.py
+++ b/solution.py
@@ -10,6 +10,7 @@
 BLK = 64
 MESH = pl.DeviceIdType.MESH
 NCH = 4
+HALF = NCH // 2
 
 
 def expand_blocks(block_mask, width):
@@ -47,11 +48,12 @@
     return (updated.astype(jnp.bfloat16), occupations)
 
 
-def kernel(order_total, p_ref, pat_ref, out_ref, occ_ref, arow, bcol, acc, xa, xb, tz, tp, tsum,
+def kernel(order_total, p_ref, pat_hbm, out_ref, occ_ref, arow, bcol, acc, xa, xb, tz, tp, tsum, pat_ref, mask, in_s,
            mid_s, mid_r, inn_s, inn_r, edge_s, edge_r, dia_s, xa_r, xb_r, fa_s, fb_s,
            x_s, x_r, y_s, y_r, s_s, s_r, tz_s, tz_r, tp_s, tp_r):
     rows, cols = p_ref.shape
     ch = rows // NCH
+    mrows = 128
     half = cols // 2
     r = lax.axis_index("row")
     c = lax.axis_index("col")
@@ -74,6 +76,13 @@
     def blk(b):
         return b + flip * (3 - 2 * b)
 
+    own_in = pltpu.make_async_copy(p_ref, arow.at[c], in_s.at[0])
+    own_in.start()
+    own_b = pltpu.make_async_copy(p_ref, bcol.at[r], in_s.at[1])
+    own_b.start()
+    pat_in = pltpu.make_async_copy(pat_hbm, pat_ref, in_s.at[2])
+    pat_in.start()
+
     barrier = pltpu.get_barrier_semaphore()
     for d in range(1, 8):
         pl.semaphore_signal(barrier, inc=1, device_id=((r + d) % 8, c), device_id_type=MESH)
@@ -174,10 +183,10 @@
         return send(p_ref.at[piece(k)], bcol.at[r, piece(k)], y_s.at[k], y_r.at[k], (yn, c))
 
     def y_fwd(k):
-        return send(bcol.at[xn, piece(k)], bcol.at[xn, piece(k)], y_s.at[4 + k], y_r.at[4 + k], (yn, c))
+        return send(bcol.at[xn, piece(k)], bcol.at[xn, piece(k)], y_s.at[NCH + k], y_r.at[NCH + k], (yn, c))
 
     def x_fwd(k):
-        return send(bcol.at[yn, piece(k)], bcol.at[yn, piece(k)], x_s.at[2 + k], x_r.at[2 + k], (xn, c))
+        return send(bcol.at[yn, piece(k)], bcol.at[yn, piece(k)], x_s.at[HALF + k], x_r.at[HALF + k], (xn, c))
 
     def sib_fwd(slot, k, pos, own=False):
         src = p_ref if own else bcol.at[slot]
@@ -194,22 +203,22 @@
             edge(1, k, start)
 
         x_own(k).start()
-        y_own((k + 2) % NCH).start()
+        y_own((k + HALF) % NCH).start()
     for k in range(NCH):
         sib_fwd(r, k, k, True).start()
 
     def part(i, carry):
         tpp, tcc = carry
         at = pl.multiple_of(i * 64, 64)
-        v = p_ref[pl.ds(at, 64), :]
-        arow[c, pl.ds(at, 64), :] = v
-        bcol[r, pl.ds(at, 64), :] = v
-        w = v.astype(jnp.float32)
+        w = arow[c, pl.ds(at, 64), :].astype(jnp.float32)
         gr = lax.broadcasted_iota(jnp.int32, w.shape, 0) + (r * rows + at)
         gc = lax.broadcasted_iota(jnp.int32, w.shape, 1) + c * cols
         dpart = jnp.where(gr == gc, w, 0.0)
         return tpp + jnp.sum(dpart, axis=0, keepdims=True), tcc + jnp.sum(w * w, axis=0, keepdims=True)
 
+    own_in.wait()
+    own_b.wait()
+    pat_in.wait()
     zero = jnp.zeros((1, cols), jnp.float32)
     tpp, tcc = lax.fori_loop(0, rows // 64, part, (zero, zero))
     which = lax.broadcasted_iota(jnp.int32, (8, 128), 0)
@@ -227,27 +236,27 @@
         got(arow.at[blk(b), piece(i % NCH)], mid_r.at[i])
         edge(b, i % NCH, start)
 
-    for i in range(6):
-        if i < 4:
-            kx, ky = i, (i + 2) % NCH
+    for i in range(NCH + HALF):
+        if i < NCH:
+            kx, ky = i, (i + HALF) % NCH
             got(bcol.at[xn, piece(kx)], x_r.at[kx])
-            if kx < 2:
+            if kx < HALF:
                 y_fwd(kx).start()
-            sib_fwd(xn, kx, 4 + kx).start()
+            sib_fwd(xn, kx, NCH + kx).start()
             got(bcol.at[yn, piece(ky)], y_r.at[ky])
-            if ky >= 2:
+            if ky >= HALF:
                 x_fwd(ky).start()
-            sib_fwd(yn, ky, 8 + ky).start()
+            sib_fwd(yn, ky, 2 * NCH + ky).start()
 
             @pl.when(is_mid & (role == 0))
             def _():
                 dia(ky).start()
         else:
-            k = i - 4
-            got(bcol.at[dg, piece(2 + k)], x_r.at[4 + k])
-            sib_fwd(dg, 2 + k, 14 + k).start()
-            got(bcol.at[dg, piece(k)], y_r.at[4 + k])
-            sib_fwd(dg, k, 12 + k).start()
+            k = i - NCH
+            got(bcol.at[dg, piece(HALF + k)], x_r.at[NCH + k])
+            sib_fwd(dg, HALF + k, 3 * NCH + HALF + k).start()
+            got(bcol.at[dg, piece(k)], y_r.at[NCH + k])
+            sib_fwd(dg, k, 3 * NCH + k).start()
 
         @pl.when(is_mid)
         def _():
@@ -257,38 +266,54 @@
         def _():
             edge_got(1 + i // NCH, i % NCH)
 
-        if i >= 1 and i < 5:
-            kd = (i + 1) % NCH
+        if i >= 1 and i <= NCH:
+            kd = (i - 1 + HALF) % NCH
 
             @pl.when(is_end & (role == 0))
             def _():
                 got(xa.at[piece(kd)], xa_r.at[kd])
                 dia_x(kd).start()
                 dia_y(kd).start()
-        if i == 1:
-            for t in tz_out:
-                t.wait_send()
-            for d in range(1, 4):
-                got(tz.at[(c + 4 - d) % 4], tz_r.at[d])
-            tp[r] = ((tz[0] + tz[1]) + tz[2]) + tz[3]
-            for t in tp_out:
-                t.start()
+
+    def traces():
+        for d in range(1, 4):
+            got(tz.at[(c + 4 - d) % 4], tz_r.at[d])
+        tp[r] = ((tz[0] + tz[1]) + tz[2]) + tz[3]
+        for t in tp_out:
+            t.start()
 
     sx, sy, sd = xn + 1 - 2 * core, yn + 1 - 2 * core, dg + 1 - 2 * core
-    for slot, base in ((sib, 0), (sx, 4), (sy, 8), (sd, 12)):
+    for slot, base in ((sib, 0), (sx, NCH), (sy, 2 * NCH), (sd, 3 * NCH)):
         for k in range(NCH):
             got(bcol.at[slot, piece(k)], s_r.at[base + k])
 
-    def mm(b, h, first=False):
+    def mm(b, h, first=False, only=None):
         slot = blk(b)
 
         def some(k, _):
-            rr = piece(k)
+            rr = pl.ds(k * mrows, mrows) if isinstance(k, int) else pl.ds(pl.multiple_of(k * mrows, mrows), mrows)
             v = jnp.dot(arow[slot, rr, lane(h)], bcol[2 * slot + h], preferred_element_type=jnp.float32)
             acc[rr, :] = v if first else acc[rr, :] + v
             return 0
 
-        lax.fori_loop(0, NCH, some, 0)
+        if only is None:
+            lax.fori_loop(0, rows // mrows, some, 0)
+        else:
+            some(only, 0)
+
+    def totals():
+        for d in range(1, 8):
+            got(tp.at[(r + 8 - d) % 8], tp_r.at[d])
+        tot = tp[0]
+        for d in range(1, 8):
+            tot = tot + tp[d]
+        tsum[...] = tot
+        sel = lax.broadcasted_iota(jnp.int32, (8, 128), 1) == 0
+        trace_p = jnp.sum(jnp.where(sel & (which == 0), tot, 0.0))
+        trace_c = jnp.sum(jnp.where(sel & (which == 1), tot, 0.0))
+        take = trace_p > 1.0 * order_total
+        occ_ref[0] = trace_p / order_total
+        occ_ref[1] = jnp.where(take, trace_c, 2.0 * trace_p - trace_c) / order_total
 
     def mm_all(b):
         lax.fori_loop(0, 2, lambda h, _: (mm(b, h), 0)[1], 0)
@@ -297,22 +322,31 @@
         for k in range(NCH):
             arow[blk(b), :, pl.ds(pl.multiple_of(h * half + k * ch, ch), ch)] = src(k).T
 
+    nbr, nbc = pat_ref.shape
+    spread = (lax.broadcasted_iota(jnp.int32, (nbc, cols), 1) // BLK
+              == lax.broadcasted_iota(jnp.int32, (nbc, cols), 0)).astype(jnp.float32)
+    mask[...] = jnp.dot(pat_ref[...].astype(jnp.float32), spread, preferred_element_type=jnp.float32)
+
     @pl.when(is_mid)
     def _():
-        mid_step(6)
+        for i in range(NCH + HALF, 2 * NCH - 1):
+            mid_step(i)
         mm(1, 0, True)
         mm(1, 1)
-        mid_step(7)
         mm_all(0)
+        traces()
+        mid_step(2 * NCH - 1)
+        totals()
         mm_all(2)
         mm_all(3)
 
     @pl.when(is_end)
     def _():
-        edge_got(2, 2)
         mm(0, 0, True)
         mm(0, 1)
-        edge_got(2, 3)
+        for k in range(HALF, NCH):
+            edge_got(2, k)
+        traces()
 
         @pl.when(role == 0)
         def _():
@@ -323,6 +357,7 @@
                 return 0
 
             lax.fori_loop(0, 6, slab, 0)
+            totals()
 
         def all_xa():
             for k in range(NCH):
@@ -348,16 +383,36 @@
             all_xb()
             turn(lambda k: xb[piece(k), :], 3, other)
 
+        per = mrows // ch
+
         @pl.when((role == 1) | (role == 2))
         def _():
             mm_all(1)
-            edge_got(3, 0)
-            mm_all(2)
-            edge_got(3, 1)
             mm(3, other)
-            edge_got(3, 2)
-            edge_got(3, 3)
-            mm(3, zhalf)
+            for k in range(HALF):
+                edge_got(3, k)
+            mm(2, 0)
+            for k in range(HALF, NCH - 1):
+                edge_got(3, k)
+            mm(2, 1)
+            totals()
+            for k in range(3):
+                mm(3, zhalf, only=k)
+            edge_got(3, NCH - 1)
+            mm(3, zhalf, only=3)
+
+        def mm_part(b, h, src, sem, g):
+            deep = half // 2
+            for k in range(g * HALF, (g + 1) * HALF):
+                got(src.at[piece(k)], sem.at[k])
+            v = src[pl.ds(g * deep, deep), :].T
+            slot = blk(b)
+            depth = pl.ds(g * deep, deep)
+
+            for m in range(rows // mrows):
+                rr = pl.ds(m * mrows, mrows)
+                acc[rr, :] += jnp.dot(v[m * mrows:(m + 1) * mrows, :], bcol[2 * slot + h, depth, :],
+                                      preferred_element_type=jnp.float32)
 
         @pl.when(role == 3)
         def _():
@@ -365,48 +420,33 @@
             mm(2, zhalf)
             for k in range(NCH):
                 edge_got(3, k)
-            mm_all(3)
-            all_xa()
-            turn(lambda k: xa[piece(k), :], 1, other)
-            mm(1, other)
-            all_xb()
-            turn(lambda k: xb[piece(k), :], 2, other)
-            mm(2, other)
-
-    for t in tp_out:
-        t.wait_send()
-    for d in range(1, 8):
-        got(tp.at[(r + 8 - d) % 8], tp_r.at[d])
-    tot = tp[0]
-    for d in range(1, 8):
-        tot = tot + tp[d]
-    tsum[...] = tot
-    sel = lax.broadcasted_iota(jnp.int32, (8, 128), 1) == 0
-    trace_p = jnp.sum(jnp.where(sel & (which == 0), tot, 0.0))
-    trace_c = jnp.sum(jnp.where(sel & (which == 1), tot, 0.0))
-    take = trace_p > 1.0 * order_total
-    occ_ref[0] = trace_p / order_total
-    occ_ref[1] = jnp.where(take, trace_c, 2.0 * trace_p - trace_c) / order_total
+                if (k + 1) % per == 0:
+                    mm(3, 0, only=k // per)
+                    mm(3, 1, only=k // per)
+                if k == NCH - 2:
+                    mm_part(1, other, xa, xa_r, 0)
+                    mm_part(2, other, xb, xb_r, 0)
+                    totals()
+            mm_part(1, other, xa, xa_r, 1)
+            mm_part(2, other, xb, xb_r, 1)
+
     takev = tsum[0:1, 0:1] > 1.0 * order_total
-
-    nbr, nbc = pat_ref.shape
-    spread = (lax.broadcasted_iota(jnp.int32, (nbc, cols), 1) // BLK
-              == lax.broadcasted_iota(jnp.int32, (nbc, cols), 0)).astype(jnp.float32)
-    mask = jnp.dot(pat_ref[...].astype(jnp.float32), spread, preferred_element_type=jnp.float32)
     for b in range(nbr):
         rr = pl.ds(b * BLK, BLK)
         m = mask[b:b + 1, :]
         sq = acc[rr, :] * m
-        alt = m * (2.0 * p_ref[rr, :].astype(jnp.float32) - sq)
+        alt = m * (2.0 * arow[c, rr, :].astype(jnp.float32) - sq)
         out_ref[rr, :] = jnp.where(takev, sq, alt).astype(jnp.bfloat16)
 
+    for t in tz_out + tp_out:
+        t.wait_send()
     for k in range(NCH):
         x_own(k).wait_send()
         y_own(k).wait_send()
-    for k in range(2):
+    for k in range(HALF):
         y_fwd(k).wait_send()
-        x_fwd(2 + k).wait_send()
-    for pos in range(16):
+        x_fwd(HALF + k).wait_send()
+    for pos in range(4 * NCH):
         sib_fwd(r, 0, pos, True).wait_send()
 
     @pl.when(is_mid)
@@ -453,7 +493,7 @@
         functools.partial(kernel, order_total),
         out_shape=(jax.ShapeDtypeStruct((rows, cols), jnp.bfloat16),
                    jax.ShapeDtypeStruct((2,), jnp.float32)),
-        in_specs=[pl.BlockSpec(memory_space=pltpu.VMEM)] * 2,
+        in_specs=[pl.BlockSpec(memory_space=pltpu.HBM)] * 2,
         out_specs=(pl.BlockSpec(memory_space=pltpu.VMEM), pl.BlockSpec(memory_space=pltpu.SMEM)),
         scratch_shapes=[
             pltpu.VMEM((4, rows, cols), jnp.bfloat16),
@@ -464,10 +504,13 @@
             pltpu.VMEM((4, 8, 128), jnp.float32),
             pltpu.VMEM((8, 8, 128), jnp.float32),
             pltpu.VMEM((8, 128), jnp.float32),
-            dma((8,)), dma((8,)), dma((4,)), dma((4,)), dma((12,)), dma((12,)),
-            dma((4,)), dma((4,)), dma((4,)), dma((4,)), dma((4,)),
-            dma((6,)), dma((6,)), dma((6,)), dma((6,)),
-            dma((16,)), dma((16,)),
+            pltpu.VMEM(pattern.shape, jnp.int32),
+            pltpu.VMEM((pattern.shape[0], cols), jnp.float32),
+            dma((3,)),
+            dma((2 * NCH,)), dma((2 * NCH,)), dma((NCH,)), dma((NCH,)), dma((3 * NCH,)), dma((3 * NCH,)),
+            dma((NCH,)), dma((NCH,)), dma((NCH,)), dma((NCH,)), dma((NCH,)),
+            dma((NCH + HALF,)), dma((NCH + HALF,)), dma((NCH + HALF,)), dma((NCH + HALF,)),
+            dma((4 * NCH,)), dma((4 * NCH,)),
             dma((4,)), dma((4,)), dma((8,)), dma((8,)),
         ],
         compiler_params=pltpu.CompilerParams(

time: 75.5 us -> 74.8 us (level)
  Pallas kernels: 71.3 us -> 70.5 us
where the time goes in v3:
time: 74.8 us; the launch traced here: 74.6 us
  Pallas kernels  70.5 us (94%)
  local copies, waits for them, and re-layouts  3.39 us (5%)
    pallas_call x1, Pallas kernels, body(): pl.pallas_call(functools.partial(kernel, order_total), out_shape=(jax.Sha...  70.5 us
    unnamed x6, local copies, waits for them, and re-layouts  3.39 us

profile of v3, /device:TPU:7, one launch (start us, length us, event | category | flops | bytes accessed | tf_op | source)
XLA Modules:
  0.0 74.6 jit_solution(6387473572276568884)
XLA Ops:
  0.6 0.0 copy-start
  0.6 1.2 %copy-done = bf16[512,1024]{1,0:T(8,128)(2,1)S(1)} copy-done((bf16[512,1024]{1,0:T(8,128)(2,1)S(1)}, bf16[512,1024]{1,0:T(8,128)(2,1)}, u32[]{:S(2)}) %copy-start) | copy-done | bytes 1048600
  1.9 0.0 copy-start.1
  1.9 0.7 copy-done.1
  2.5 70.5 %shard_map.41 = (bf16[512,1024]{1,0:T(8,128)(2,1)S(1)}, f32[2]{0:T(128)S(1)}) custom-call(bf16[512,1024]{1,0:T(8,128)(2,1)S(1)} %copy-done, s32[8,16]{1,0:T(8,128)S(1)} %copy-done.1), custom_call_target="tpu_custom_call" | custom-call | tf_op jit(solution)/shard_map/pallas_call | solution.py:492
  73.1 1.0 %copy.6 = bf16[512,1024]{1,0:T(8,128)(2,1)} copy(bf16[512,1024]{1,0:T(8,128)(2,1)S(1)} %get-tuple-element.4) | data formatting | bytes 2097152
  74.1 0.5 copy.7
Async XLA Ops:
  0.6 1.2 %copy-start = (bf16[512,1024]{1,0:T(8,128)(2,1)S(1)}, bf16[512,1024]{1,0:T(8,128)(2,1)}, u32[]{:S(2)}) copy-start(bf16[512,1024]{1,0:T(8,128)(2,1)} %p_ref.1) | copy-start | bytes 3145732
  1.9 0.7 copy-start.1

commit v4 on v3

--- a/solution.py
+++ b/solution.py
@@ -237,6 +237,14 @@
         edge(b, i % NCH, start)
 
     for i in range(NCH + HALF):
+        @pl.when(is_mid)
+        def _():
+            mid_step(i)
+
+        @pl.when(is_end)
+        def _():
+            edge_got(1 + i // NCH, i % NCH)
+
         if i < NCH:
             kx, ky = i, (i + HALF) % NCH
             got(bcol.at[xn, piece(kx)], x_r.at[kx])
@@ -257,14 +265,6 @@
             sib_fwd(dg, HALF + k, 3 * NCH + HALF + k).start()
             got(bcol.at[dg, piece(k)], y_r.at[NCH + k])
             sib_fwd(dg, k, 3 * NCH + k).start()
-
-        @pl.when(is_mid)
-        def _():
-            mid_step(i)
-
-        @pl.when(is_end)
-        def _():
-            edge_got(1 + i // NCH, i % NCH)
 
         if i >= 1 and i <= NCH:
             kd = (i - 1 + HALF) % NCH

time: 74.8 us -> 75.1 us (level)
  no operation moved by 1% of the time
where the time goes in v4:
time: 75.1 us; the launch traced here: 74.9 us
  Pallas kernels  70.9 us (94%)
  local copies, waits for them, and re-layouts  3.39 us (5%)
    pallas_call x1, Pallas kernels, body(): pl.pallas_call(functools.partial(kernel, order_total), out_shape=(jax.Sha...  70.9 us
    unnamed x6, local copies, waits for them, and re-layouts  3.39 us

profile of v4, /device:TPU:7, one launch (start us, length us, event | category | flops | bytes accessed | tf_op | source)
XLA Modules:
  0.0 74.9 jit_solution(14853800566848360205)
XLA Ops:
  0.6 0.0 copy-start
  0.6 1.2 %copy-done = bf16[512,1024]{1,0:T(8,128)(2,1)S(1)} copy-done((bf16[512,1024]{1,0:T(8,128)(2,1)S(1)}, bf16[512,1024]{1,0:T(8,128)(2,1)}, u32[]{:S(2)}) %copy-start) | copy-done | bytes 1048600
  1.9 0.0 copy-start.1
  1.9 0.7 copy-done.1
  2.5 70.9 %shard_map.41 = (bf16[512,1024]{1,0:T(8,128)(2,1)S(1)}, f32[2]{0:T(128)S(1)}) custom-call(bf16[512,1024]{1,0:T(8,128)(2,1)S(1)} %copy-done, s32[8,16]{1,0:T(8,128)S(1)} %copy-done.1), custom_call_target="tpu_custom_call" | custom-call | tf_op jit(solution)/shard_map/pallas_call | solution.py:492
  73.5 1.0 %copy.6 = bf16[512,1024]{1,0:T(8,128)(2,1)} copy(bf16[512,1024]{1,0:T(8,128)(2,1)S(1)} %get-tuple-element.4) | data formatting | bytes 2097152
  74.4 0.5 copy.7
Async XLA Ops:
  0.6 1.2 %copy-start = (bf16[512,1024]{1,0:T(8,128)(2,1)S(1)}, bf16[512,1024]{1,0:T(8,128)(2,1)}, u32[]{:S(2)}) copy-start(bf16[512,1024]{1,0:T(8,128)(2,1)} %p_ref.1) | copy-start | bytes 3145732
  1.9 0.7 copy-start.1
